TPU v7x, 32 devices: a whole 2x2x4 slice. The times are simulated.
32 devices in a mesh: tm: 2 (over core), height: 8 (over z, y), head: 2 (over x).
Axes of the slice: x: 2, y: 2, z: 4, core: 2. Of those that a mesh axis runs over, the one named last changes fastest.
Arguments:
- queries: bfloat16 [4, 16, 64, 1280], P('tm', 'height', None, 'head'), may hold values from -22 to 22
- keys_values: bfloat16 [2, 4, 16, 64, 1280], P(None, 'tm', 'height', None, 'head'), may hold values from -7 to 7
- out_weight: bfloat16 [1280, 5120], P('head'), may hold values from -0.15625 to 0.15625
Outputs:
- mixed: bfloat16 [64, 4, 16, 5120], P('head', 'tm', 'height')
All inputs are finite; a program needn't handle non-finite values.
Results may differ from a plain program's by a relative error of at most 0.013.
Values may be sent and summed in bfloat16 or wider, within the bound.
A program may use at most 128 MiB of HBM per device.

v0:
```python
import math
import jax
import jax.numpy as jnp
from jax import lax
from jax.sharding import PartitionSpec as P

HD = 128
TILE = 16
WINDOW = 3
PAD_ROWS = 2
VALID_COLS = 52
masked_value = -1e30


def from_partner(value, axis, apart):
    mask = 2**apart
    pairs = [(source, source ^ mask) for source in range(lax.axis_size(axis))]
    return lax.ppermute(value, axis, pairs)


def window_start(tile_index, tile_count):
    span_size = min(tile_count, WINDOW)
    return (jnp.clip(tile_index - 1, 0, tile_count - span_size), span_size)


def column_groups(col_tiles):
    col_span = min(col_tiles, WINDOW)
    grouped = []
    for col_tile in range(col_tiles):
        key_begin = max(0, min(col_tile - 1, col_tiles - col_span))
        if len(grouped) > 0 and grouped[-1][2] == key_begin:
            grouped[-1] = (grouped[-1][0], col_tile + 1, key_begin)
        else:
            grouped.append((col_tile, col_tile + 1, key_begin))
    return (grouped, col_span)


def edge_frame(local_keys, side_index):
    last_frame = local_keys.shape[1] - 1
    begin = (1 - side_index) * last_frame
    return lax.dynamic_slice_in_dim(local_keys, begin, 1, 1)


def attach_rim(local_keys, rim_frame, side_index):
    joined = jnp.concatenate([rim_frame, local_keys, rim_frame], axis=1)
    begin = 1 - side_index
    return lax.dynamic_slice_in_dim(joined, begin, local_keys.shape[1] + 1, 1)


def on_device(queries, keys_values, out_weight):
    frames_dev, rows_dev, col_count, width_dev = queries.shape
    heads_dev = width_dev // HD
    frame_count = frames_dev * lax.axis_size("tm")
    frame_rows = rows_dev * lax.axis_size("height")
    valid_rows = frame_rows - PAD_ROWS
    row_tiles = frame_rows // TILE
    side_index = lax.axis_index("tm")
    first_frame = side_index * frames_dev
    first_row = lax.axis_index("height") * rows_dev
    score_scale = 1.0 / math.sqrt(HD)
    query_frames = first_frame + jnp.arange(frames_dev, dtype=jnp.int32)
    frame_low, frame_span = window_start(query_frames, frame_count)
    query_rows = first_row + jnp.arange(rows_dev, dtype=jnp.int32)
    row_tile_low, row_span = window_start(query_rows // TILE, row_tiles)
    row_low = row_tile_low * TILE
    row_high = row_low + row_span * TILE
    grouped, col_span = column_groups(col_count // TILE)
    key_width = col_span * TILE
    query_groups = []
    col_fits = []
    starters = []
    for first_tile, last_tile, key_tile in grouped:
        selected = queries[:, :, first_tile * TILE : last_tile * TILE, :]
        query_groups.append(selected.reshape(-1, width_dev))
        col_fits.append(key_tile * TILE + jnp.arange(key_width, dtype=jnp.int32) < VALID_COLS)
        query_total = selected.shape[0] * selected.shape[1] * selected.shape[2]
        starters.append(
            tuple(
                (
                    (
                        jnp.full((query_total,), masked_value, jnp.float32),
                        jnp.zeros((query_total,), jnp.float32),
                        jnp.zeros((query_total, HD), jnp.float32),
                    )
                    for member in range(heads_dev)
                )
            )
        )
    initial = tuple(starters)
    whole_rows = lax.all_gather(keys_values, "height", axis=2, tiled=True)
    rim_frame = from_partner(edge_frame(whole_rows, side_index), "tm", 0)
    with_rims = attach_rim(whole_rows, rim_frame, side_index)
    extended = with_rims.shape[1]
    row_piece = with_rims.shape[2]
    key_frames = first_frame - side_index + jnp.arange(extended, dtype=jnp.int32)
    key_rows = jnp.arange(row_piece, dtype=jnp.int32)
    time_fits = (key_frames[None, :] >= frame_low[:, None]) & (
        key_frames[None, :] < frame_low[:, None] + frame_span
    )
    row_fits = (key_rows[None, :] >= row_low[:, None]) & (key_rows[None, :] < row_high[:, None])
    row_fits = row_fits & (key_rows[None, :] < valid_rows)
    updated = []
    for add_group_id, (add_first_tile, add_last_tile, add_key_tile) in enumerate(grouped):
        add_query_cols = (add_last_tile - add_first_tile) * TILE
        visible = (
            time_fits[:, None, None, :, None, None]
            & row_fits[None, :, None, None, :, None]
            & col_fits[add_group_id][None, None, None, None, None, :]
        )
        visible = jnp.broadcast_to(
            visible, (frames_dev, rows_dev, add_query_cols, extended, row_piece, key_width)
        )
        visible = visible.reshape(
            frames_dev * rows_dev * add_query_cols, extended * row_piece * key_width
        )
        col_begin = add_key_tile * TILE
        key_block = with_rims[0, :, :, col_begin : col_begin + key_width, :].reshape(-1, width_dev)
        value_block = with_rims[1, :, :, col_begin : col_begin + key_width, :].reshape(
            -1, width_dev
        )
        head_states = []
        for member in range(heads_dev):
            running_max, running_sum, running_out = initial[add_group_id][member]
            head_query = query_groups[add_group_id][:, member * HD : (member + 1) * HD]
            head_keys = key_block[:, member * HD : (member + 1) * HD]
            head_values = value_block[:, member * HD : (member + 1) * HD]
            scores = (
                jnp.einsum("qd,kd->qk", head_query, head_keys, preferred_element_type=jnp.float32)
                * score_scale
            )
            scores = jnp.where(visible, scores, masked_value)
            new_max = jnp.maximum(running_max, jnp.max(scores, axis=1))
            weights = jnp.where(visible, jnp.exp(scores - new_max[:, None]), 0.0)
            new_sum = jnp.sum(weights, axis=1)
            new_out = jnp.dot(
                weights.astype(jnp.bfloat16), head_values, preferred_element_type=jnp.float32
            )
            head_states.append((new_max, new_sum, new_out))
        updated.append(tuple(head_states))
    final_state = tuple(updated)
    pieces = []
    for group_id, (first_tile, last_tile, key_tile) in enumerate(grouped):
        query_cols = (last_tile - first_tile) * TILE
        head_parts = [state[2] / state[1][:, None] for state in final_state[group_id]]
        group_out = jnp.concatenate(head_parts, axis=1).astype(jnp.bfloat16)
        group_out = group_out.reshape(frames_dev, rows_dev, query_cols, width_dev)
        pieces.append(jnp.transpose(group_out, (2, 0, 1, 3)))
    attended = jnp.concatenate(pieces, axis=0)
    return lax.psum_scatter(
        jnp.einsum(
            "cfrh,hd->cfrd", attended, out_weight, preferred_element_type=jnp.float32
        ).astype(jnp.bfloat16),
        "head",
        scatter_dimension=0,
        tiled=True,
    )


def solution(mesh):
    placed = (
        P("tm", "height", None, "head"),
        P(None, "tm", "height", None, "head"),
        P("head", None),
    )
    return jax.shard_map(
        on_device,
        mesh=mesh,
        in_specs=placed,
        out_specs=P("head", "tm", "height", None),
        check_vma=False,
    )
```

profile of v0, /device:TPU:0, one launch (start us, length us, event | category | flops | bytes accessed | tf_op | source)
XLA Modules:
  0.0 177.9 jit_solution(4382157549609009276)
XLA Ops:
  6.5 0.7 all-gather.2.cloned.1.call-update
  7.3 91.2 %all-gather.2.cloned.1.call-done = bf16[2,2,16,64,640]{4,3,2,1,0:T(8,128)(2,1)} async-done(((bf16[2,2,2,64,640]{4,3,2,1,0:T(8,128)(2,1)}), bf16[2,2,16,64,640]{4,3,2,1,0:T(8,128)(2,1)}) %all-gather.2.cloned.1.call-update) | async-done | bytes 5242896 | tf_op jit(solution)/shard_map/all_gather | solution.py:90
  98.6 3.5 %constant_dynamic-slice_fusion = bf16[2,1,16,64,640]{4,3,2,1,0:T(8,128)(2,1)} fusion(bf16[2,2,16,64,640]{4,3,2,1,0:T(8,128)(2,1)} %all-gather.2.cloned.1.call-done, s32[]{:T(128)S(6)} %select_n.80), kind=kLoop, calls=%fused_computation.160 | loop fusion | bytes 5242884 | tf_op jit(solution)/shard_map/dynamic_slice | solution.py:41
  102.7 1.5 reshape.255
  104.8 1.5 reshape.257
  106.8 0.5 collective-permute-done
  107.3 5.7 %fusion.1 = bf16[2,3,16,64,640]{4,3,2,1,0:T(8,128)(2,1)S(1)} fusion(s32[]{:T(128)S(6)} %select_n.81, bf16[2,1,16,64,640]{4,3,2,1,0:T(8,128)(2,1)} %collective-permute-done, bf16[2,2,16,64,640]{4,3,2,1,0:T(8,128)(2,1)} %all-gather.2.cloned.1.call-done), kind=kLoop, calls=%fused_computation.4 | loop fusion | flops 7864320 | bytes 15728644 | tf_op jit(solution)/shard_map/concatenate | solution.py:45
  113.1 1.7 fusion.131
  114.8 0.5 fusion.139
  115.3 0.5 fusion.140
  115.8 0.5 fusion.141
  116.2 0.5 fusion.142
  116.7 0.5 fusion.138
  117.2 0.5 fusion.134
  117.7 0.5 fusion.135
  118.2 0.5 fusion.136
  118.7 0.5 fusion.137
  119.2 0.5 fusion.133
  119.7 1.1 fusion.45
  123.2 1.1 fusion.55
  126.9 0.6 slice-done.1
  127.5 3.8 %fusion.4 = bf16[64,2,2,5120]{3,0,2,1:T(8,128)(2,1)} fusion(bf16[640,5120]{1,0:T(8,128)(2,1)S(1)} %bitcast.112, bf16[32,2,2,640]{3,0,2,1:T(8,128)(2,1)S(1)} %bitcast.110, bf16[32,2,2,640]{3,0,2,1:T(8,128)(2,1)S(1)} %bitcast.109), kind=kOutput, calls=%fused_computation.7 | convolution fusion | flops 1679687680 | bytes 9502720 | tf_op jit(solution)/shard_map/cfrh,hd->cfrd/dot_general | solution.py:150
  131.2 36.1 %reduce-scatter.2.cloned.1.call-done = bf16[32,2,2,5120]{3,0,2,1:T(8,128)(2,1)} async-done(((bf16[64,2,2,5120]{3,0,2,1:T(8,128)(2,1)}), bf16[32,2,2,5120]{3,0,2,1:T(8,128)(2,1)}) %reduce-scatter.2.cloned.1.call-update) | async-done | bytes 1310736 | tf_op jit(solution)/shard_map/reduce_scatter | solution.py:149
  167.4 3.7 %copy.25 = bf16[32,2,2,5120]{3,2,1,0:T(2,128)(2,1)} copy(bf16[32,2,2,5120]{3,0,2,1:T(8,128)(2,1)} %reduce-scatter.2.cloned.1.call-done) | data formatting | bytes 2621440 | tf_op jit(solution)/shard_map/reduce_scatter | solution.py:149
  (54 shorter events, 6.5 us)
Async XLA Ops:
  6.5 92.0 %all-gather.2.cloned.1.call-start = ((), (), s32[]{:S(2)}) async-start(), calls=%async_computation.1 | async-start | bytes 5898240 | tf_op jit(solution)/shard_map/all_gather | solution.py:90
  7.3 160.1 %reduce-scatter.2.cloned.1.call-start = ((), (), s32[]{:S(2)}) async-start(), calls=%async_computation.2 | async-start | bytes 3932160 | tf_op jit(solution)/shard_map/reduce_scatter | solution.py:149
  102.1 5.3 %collective-permute-start = (bf16[2,1,16,64,640]{4,3,2,1,0:T(8,128)(2,1)}, bf16[2,1,16,64,640]{4,3,2,1,0:T(8,128)(2,1)}, u32[]{:S(2)}, u32[]{:S(2)}) collective-permute-start(bf16[2,1,16,64,640]{4,3,2,1,0:T(8,128)(2,1)} %constant_dynamic-slice_fusion), channel_id=1, source_target_pairs={{0,16},{16,0},{1,17},{17,1},{2,18},{18,2},{3,19},{19,3},{4,20},{20... | collective-permute-start | bytes 7864328 | tf_op jit(solution)/shard_map/ppermute | solution.py:18
  104.6 2.1 %copy-start = (bf16[2,2,64,640]{3,2,1,0:T(8,128)(2,1)S(1)}, bf16[2,2,64,640]{3,2,1,0:T(8,128)(2,1)}, u32[]{:S(2)}) copy-start(bf16[2,2,64,640]{3,2,1,0:T(8,128)(2,1)} %param.3) | copy-start | bytes 983044
  124.3 2.6 %slice-start = ((s8[6553600]{0:T(1024)(128)(4,1)}), s8[4194304]{0:T(1024)(128)(4,1)S(1)}, s32[]{:S(2)}) async-start(s8[6553600]{0:T(1024)(128)(4,1)} %bitcast.111), calls=%async_computation.3 | async-start | bytes 8388608
  125.2 2.2 %slice-start.1 = ((s8[6553600]{0:T(1024)(128)(4,1)}), s8[2359296]{0:T(1024)(128)(4,1)S(1)}, s32[]{:S(2)}) async-start(s8[6553600]{0:T(1024)(128)(4,1)} %bitcast.111), calls=%async_computation.4 | async-start | bytes 4718592
Sparse Core Ops, SparseCore 0:
  9.5 88.9 all-gather.1
  131.4 35.9 reduce-scatter.1
where the time goes:
time: 178 us
  waiting for transfers between devices  129 us (72%)
  local copies, waits for them, and re-layouts  13.9 us (8%)
  between operations  13.7 us (8%)
  matrix products  13.4 us (8%)
  other arithmetic  8.24 us (5%)
    all_gather x1, waiting for transfers between devices, on_device(): whole_rows = lax.all_gather(keys_values, 'height', axis=2, tiled=True)  91.2 us
    reduce_scatter x1, waiting for transfers between devices, on_device(): lax.psum_scatter(jnp.einsum('cfrh,hd->cfrd', attended, out_weight, prefer...  36.1 us
    concatenate x1, other arithmetic, attach_rim(): joined = jnp.concatenate([rim_frame, local_keys, rim_frame], axis=1)  5.71 us
    dot_general x10, matrix products, on_device(): jnp.einsum('qd,kd->qk', head_query, head_keys, preferred_element_type=jnp...  4.89 us
    dot_general x10, matrix products, on_device(): jnp.dot(weights.astype(jnp.bfloat16), head_values, preferred_element_type...  4.72 us
    reshape x4, local copies, waits for them, and re-layouts, on_device(): visible.reshape(frames_dev * rows_dev * add_query_cols, extended * row_pi...  3.79 us
    dot_general x1, matrix products, on_device(): jnp.einsum('cfrh,hd->cfrd', attended, out_weight, preferred_element_type=...  3.77 us
    reduce_scatter x1, local copies, waits for them, and re-layouts, on_device(): lax.psum_scatter(jnp.einsum('cfrh,hd->cfrd', attended, out_weight, prefer...  3.72 us
  transfers between devices with their start and end apart: 3, of which 3 were waited for; matrix products, arithmetic and copies ran while one was open for 3% of the time, Pallas kernels for 0%

commit v1 on v0

--- a/solution.py
+++ b/solution.py
@@ -87,7 +87,15 @@
             )
         )
     initial = tuple(starters)
-    whole_rows = lax.all_gather(keys_values, "height", axis=2, tiled=True)
+    ways, here = (lax.axis_size("height"), lax.axis_index("height"))
+    grown, reach = (keys_values, 1)
+    while reach < ways:
+        theirs = lax.ppermute(grown, "height", [(d, d ^ reach) for d in range(ways)])
+        mine_first = jnp.concatenate([grown, theirs], axis=2)
+        theirs_first = jnp.concatenate([theirs, grown], axis=2)
+        grown = jnp.where(here & reach == 0, mine_first, theirs_first)
+        reach = 2 * reach
+    whole_rows = grown
     rim_frame = from_partner(edge_frame(whole_rows, side_index), "tm", 0)
     with_rims = attach_rim(whole_rows, rim_frame, side_index)
     extended = with_rims.shape[1]

time: 178 us -> 259 us (1.46)
  waiting for transfers between devices: 129 us -> 194 us
  other arithmetic: 8.24 us -> 16.8 us
  starting transfers between devices: 0.04 us -> 7.4 us
    ppermute x0 -> x3, waiting for transfers between devices: none -> 155 us  [on_device(): lax.ppermute(grown, 'height', [(d, d ^ reach) for d in range(ways)])]
    all_gather x1 -> x0, waiting for transfers between devices: 91.2 us -> none  [on_device(): whole_rows = lax.all_gather(keys_values, 'height', axis=2, tiled=True)]
    select_n x0 -> x3, other arithmetic: none -> 8.53 us  [on_device(): grown = jnp.where(here & reach == 0, mine_first, theirs_first)]
    ppermute x0 -> x3, starting transfers between devices: none -> 7.39 us  [on_device(): lax.ppermute(grown, 'height', [(d, d ^ reach) for d in range(ways)])]
  transfers between devices with their start and end apart: 3 -> 5, of which waited for: 3 -> 5; matrix products, arithmetic and copies ran while one was open for 3% -> 2% of each run, Pallas kernels for 0% -> 0%
where the time goes in v1:
time: 259 us
  waiting for transfers between devices  194 us (75%)
  other arithmetic  16.8 us (6%)
  between operations  13.7 us (5%)
  local copies, waits for them, and re-layouts  13.6 us (5%)
  matrix products  13.4 us (5%)
  starting transfers between devices  7.4 us (3%)
    ppermute x3, waiting for transfers between devices, on_device(): lax.ppermute(grown, 'height', [(d, d ^ reach) for d in range(ways)])  155 us
    reduce_scatter x1, waiting for transfers between devices, on_device(): lax.psum_scatter(jnp.einsum('cfrh,hd->cfrd', attended, out_weight, prefer...  38.7 us
    select_n x3, other arithmetic, on_device(): grown = jnp.where(here & reach == 0, mine_first, theirs_first)  8.53 us
    ppermute x3, starting transfers between devices, on_device(): lax.ppermute(grown, 'height', [(d, d ^ reach) for d in range(ways)])  7.39 us
    concatenate x1, other arithmetic, attach_rim(): joined = jnp.concatenate([rim_frame, local_keys, rim_frame], axis=1)  5.71 us
  transfers between devices with their start and end apart: 5, of which 5 were waited for; matrix products, arithmetic and copies ran while one was open for 2% of the time, Pallas kernels for 0%

profile of v1, /device:TPU:0, one launch (start us, length us, event | category | flops | bytes accessed | tf_op | source)
XLA Modules:
  0.0 259.1 jit_solution(15216205606600074109)
XLA Ops:
  6.5 3.0 %collective-permute-start = (bf16[2,2,2,64,640]{4,3,2,1,0:T(8,128)(2,1)}, bf16[2,2,2,64,640]{4,3,2,1,0:T(8,128)(2,1)S(1)}, u32[]{:S(2)}, u32[]{:S(2)}) collective-permute-start(bf16[2,2,2,64,640]{4,3,2,1,0:T(8,128)(2,1)} %param.4), channel_id=1, source_target_pairs={{0,2},{2,0},{4,6},{6,4},{8,10},{10,8},{12,14},{14,12},{1,3},{3,1},... | collective-permute-start | bytes 1966088 | tf_op jit(solution)/shard_map/ppermute | solution.py:93
  9.5 14.9 %collective-permute-done = bf16[2,2,2,64,640]{4,3,2,1,0:T(8,128)(2,1)S(1)} collective-permute-done((bf16[2,2,2,64,640]{4,3,2,1,0:T(8,128)(2,1)}, bf16[2,2,2,64,640]{4,3,2,1,0:T(8,128)(2,1)S(1)}, u32[]{:S(2)}, u32[]{:S(2)}) %collective-permute-start) | collective-permute-done | bytes 655392 | tf_op jit(solution)/shard_map/ppermute | solution.py:93
  24.4 1.5 maximum_select_fusion.2
  26.0 1.9 collective-permute-start.1
  27.9 28.3 %collective-permute-done.1 = bf16[2,2,4,64,640]{4,3,2,1,0:T(8,128)(2,1)} collective-permute-done((bf16[2,2,4,64,640]{4,3,2,1,0:T(8,128)(2,1)S(1)}, bf16[2,2,4,64,640]{4,3,2,1,0:T(8,128)(2,1)}, u32[]{:S(2)}, u32[]{:S(2)}) %collective-permute-start.1) | collective-permute-done | bytes 1310752 | tf_op jit(solution)/shard_map/ppermute | solution.py:93
  56.1 2.9 %maximum_select_fusion.1 = bf16[2,2,8,64,640]{4,3,2,1,0:T(8,128)(2,1)S(1)} fusion(bf16[2,2,4,64,640]{4,3,2,1,0:T(8,128)(2,1)} %collective-permute-done.1, bf16[2,2,4,64,640]{4,3,2,1,0:T(8,128)(2,1)} %copy-done.1, pred[]{:T(512)S(6)} %eq.10), kind=kLoop, calls=%fused_computation.39 | loop fusion | flops 3932160 | bytes 5242881 | tf_op jit(solution)/shard_map/jit(_where)/select_n | solution.py:96
  59.1 2.6 collective-permute-start.2
  61.6 111.8 %collective-permute-done.2 = bf16[2,2,8,64,640]{4,3,2,1,0:T(8,128)(2,1)} collective-permute-done((bf16[2,2,8,64,640]{4,3,2,1,0:T(8,128)(2,1)S(1)}, bf16[2,2,8,64,640]{4,3,2,1,0:T(8,128)(2,1)}, u32[]{:S(2)}, u32[]{:S(2)}) %collective-permute-start.2) | collective-permute-done | bytes 2621472 | tf_op jit(solution)/shard_map/ppermute | solution.py:93
  173.5 4.1 %maximum_select_fusion = bf16[2,2,16,64,640]{4,3,2,1,0:T(8,128)(2,1)S(1)} fusion(bf16[2,2,8,64,640]{4,3,2,1,0:T(8,128)(2,1)} %collective-permute-done.2, bf16[2,2,8,64,640]{4,3,2,1,0:T(8,128)(2,1)S(1)} %maximum_select_fusion.1, pred[]{:T(512)S(6)} %eq.9), kind=kLoop, calls=%fused_computation.8 | loop fusion | flops 7864320 | bytes 10485761 | tf_op jit(solution)/shard_map/jit(_where)/select_n | solution.py:96
  177.5 2.0 constant_dynamic-slice_fusion
  179.5 1.3 copy-done
  181.4 1.5 reshape.255
  183.5 1.5 reshape.257
  185.5 0.5 collective-permute-done.3
  186.0 5.7 %fusion.1 = bf16[2,3,16,64,640]{4,3,2,1,0:T(8,128)(2,1)S(1)} fusion(s32[]{:T(128)S(6)} %select_n.111, bf16[2,1,16,64,640]{4,3,2,1,0:T(8,128)(2,1)} %collective-permute-done.3, bf16[2,2,16,64,640]{4,3,2,1,0:T(8,128)(2,1)} %copy-done), kind=kLoop, calls=%fused_computation.4 | loop fusion | flops 7864320 | bytes 15728644 | tf_op jit(solution)/shard_map/concatenate | solution.py:45
  191.7 1.7 fusion.131
  193.9 0.5 fusion.140
  195.9 0.5 fusion.135
  198.4 1.1 fusion.45
  201.9 1.1 fusion.55
  205.5 0.6 slice-done.1
  206.1 3.8 %fusion.4 = bf16[64,2,2,5120]{3,0,2,1:T(8,128)(2,1)} fusion(bf16[640,5120]{1,0:T(8,128)(2,1)S(1)} %bitcast.112, bf16[32,2,2,640]{3,0,2,1:T(8,128)(2,1)S(1)} %bitcast.110, bf16[32,2,2,640]{3,0,2,1:T(8,128)(2,1)S(1)} %bitcast.109), kind=kOutput, calls=%fused_computation.7 | convolution fusion | flops 1679687680 | bytes 9502720 | tf_op jit(solution)/shard_map/cfrh,hd->cfrd/dot_general | solution.py:158
  209.9 38.7 %reduce-scatter.2.cloned.1.call-done = bf16[32,2,2,5120]{3,0,2,1:T(8,128)(2,1)} async-done(((bf16[64,2,2,5120]{3,0,2,1:T(8,128)(2,1)}), bf16[32,2,2,5120]{3,0,2,1:T(8,128)(2,1)}) %reduce-scatter.2.cloned.1.call-update) | async-done | bytes 1310736 | tf_op jit(solution)/shard_map/reduce_scatter | solution.py:157
  248.6 3.7 %copy.25 = bf16[32,2,2,5120]{3,2,1,0:T(2,128)(2,1)} copy(bf16[32,2,2,5120]{3,0,2,1:T(8,128)(2,1)} %reduce-scatter.2.cloned.1.call-done) | data formatting | bytes 2621440 | tf_op jit(solution)/shard_map/reduce_scatter | solution.py:157
  (64 shorter events, 10.4 us)
Async XLA Ops:
  6.5 242.0 %reduce-scatter.2.cloned.1.call-start = ((), (), s32[]{:S(2)}) async-start(), calls=%async_computation.1 | async-start | bytes 3932160 | tf_op jit(solution)/shard_map/reduce_scatter | solution.py:157
  6.5 17.9 %collective-permute-start = (bf16[2,2,2,64,640]{4,3,2,1,0:T(8,128)(2,1)}, bf16[2,2,2,64,640]{4,3,2,1,0:T(8,128)(2,1)S(1)}, u32[]{:S(2)}, u32[]{:S(2)}) collective-permute-start(bf16[2,2,2,64,640]{4,3,2,1,0:T(8,128)(2,1)} %param.4), channel_id=1, source_target_pairs={{0,2},{2,0},{4,6},{6,4},{8,10},{10,8},{12,14},{14,12},{1,3},{3,1},... | collective-permute-start | bytes 1966088 | tf_op jit(solution)/shard_map/ppermute | solution.py:93
  26.0 1.9 copy-start.1
  26.0 30.1 %collective-permute-start.1 = (bf16[2,2,4,64,640]{4,3,2,1,0:T(8,128)(2,1)S(1)}, bf16[2,2,4,64,640]{4,3,2,1,0:T(8,128)(2,1)}, u32[]{:S(2)}, u32[]{:S(2)}) collective-permute-start(bf16[2,2,4,64,640]{4,3,2,1,0:T(8,128)(2,1)S(1)} %maximum_select_fusion.2), channel_id=1, source_target_pairs={{0,4},{2,6},{4,0},{6,2},{8,12},{10,14},{12,8},{14,10},{1,5},{3,7},... | collective-permute-start | bytes 3932168 | tf_op jit(solution)/shard_map/ppermute | solution.py:93
  59.1 114.4 %collective-permute-start.2 = (bf16[2,2,8,64,640]{4,3,2,1,0:T(8,128)(2,1)S(1)}, bf16[2,2,8,64,640]{4,3,2,1,0:T(8,128)(2,1)}, u32[]{:S(2)}, u32[]{:S(2)}) collective-permute-start(bf16[2,2,8,64,640]{4,3,2,1,0:T(8,128)(2,1)S(1)} %maximum_select_fusion.1), channel_id=1, source_target_pairs={{0,8},{2,10},{4,12},{6,14},{8,0},{10,2},{12,4},{14,6},{1,9},{3,11}... | collective-permute-start | bytes 7864328 | tf_op jit(solution)/shard_map/ppermute | solution.py:93
  177.5 3.2 %copy-start = (bf16[2,2,16,64,640]{4,3,2,1,0:T(8,128)(2,1)}, bf16[2,2,16,64,640]{4,3,2,1,0:T(8,128)(2,1)S(1)}, u32[]{:S(2)}) copy-start(bf16[2,2,16,64,640]{4,3,2,1,0:T(8,128)(2,1)S(1)} %maximum_select_fusion) | copy-start | bytes 15728644
  180.8 5.3 %collective-permute-start.3 = (bf16[2,1,16,64,640]{4,3,2,1,0:T(8,128)(2,1)}, bf16[2,1,16,64,640]{4,3,2,1,0:T(8,128)(2,1)}, u32[]{:S(2)}, u32[]{:S(2)}) collective-permute-start(bf16[2,1,16,64,640]{4,3,2,1,0:T(8,128)(2,1)} %constant_dynamic-slice_fusion), channel_id=1, source_target_pairs={{0,16},{16,0},{1,17},{17,1},{2,18},{18,2},{3,19},{19,3},{4,20},{20... | collective-permute-start | bytes 7864328 | tf_op jit(solution)/shard_map/ppermute | solution.py:18
  183.3 2.1 copy-start.2
  202.9 2.6 slice-start
  203.9 2.2 slice-start.1
Sparse Core Ops, SparseCore 0:
  210.0 38.4 reduce-scatter.1
